TPU v7x, 32 devices: a whole 2x2x4 slice. The times are simulated.
32 devices in a mesh: dp: 16 (over z, y, core), tensor: 2 (over x).
Axes of the slice: x: 2, y: 2, z: 4, core: 2. Of those that a mesh axis runs over, the one named last changes fastest.
Arguments:
- tokens: bfloat16 [16384, 4096], P(('dp', 'tensor')), may hold values from -6 to 6
- out_grad: bfloat16 [16384, 2048], P('dp', 'tensor'), may hold values from -6 to 6
- weights: bfloat16 [4096, 2, 2048], P(None, None, 'tensor'), may hold values from -0.09375 to 0.09375
- master: float32 [4096, 2, 2048], P('dp', None, 'tensor'), may hold values from -0.09375 to 0.09375
- first_moment: float32 [4096, 2, 2048], P('dp', None, 'tensor'), may hold values from -4 to 4
- second_moment: float32 [4096, 2, 2048], P('dp', None, 'tensor'), may hold values from 0.05 to 5
Outputs:
- input_grad: bfloat16 [16384, 4096], P(('dp', 'tensor'))
- new_weights: bfloat16 [4096, 2, 2048], P(None, None, 'tensor')
- new_master: float32 [4096, 2, 2048], P('dp', None, 'tensor')
- new_first: float32 [4096, 2, 2048], P('dp', None, 'tensor')
- new_second: float32 [4096, 2, 2048], P('dp', None, 'tensor')
All inputs are finite; a program needn't handle non-finite values.
Results may differ from a plain program's by a relative error of at most 0.012.
Values may be sent and summed in bfloat16 or wider, within the bound.
A program may use at most 192 MiB of HBM per device.

v0:
```python
import jax
import jax.numpy as jnp
from jax import lax
from jax.sharding import PartitionSpec as P

SEQ = 512


def linear_step(earlier, latter):
    return (earlier[0] * latter[0], latter[0] * earlier[1] + latter[1])


def local_backward(projected, out_grad):
    token_count = projected.shape[0]
    hidden_width = projected.shape[1] // 2
    shaped = (token_count // SEQ, SEQ, hidden_width)
    gate_value = jax.nn.sigmoid(projected[:, :hidden_width]).reshape(shaped)
    candidate = projected[:, hidden_width:].reshape(shaped)
    upstream = out_grad.astype(jnp.float32).reshape(shaped)
    retain = 1.0 - gate_value
    _, hidden_state = lax.associative_scan(linear_step, (retain, gate_value * candidate), axis=1)
    zeros_row = jnp.zeros_like(hidden_state[:, :1])
    previous = jnp.concatenate([zeros_row, hidden_state[:, :-1]], axis=1)
    retain_next = jnp.concatenate([retain[:, 1:], zeros_row], axis=1)
    _, flipped = lax.associative_scan(
        linear_step, (jnp.flip(retain_next, axis=1), jnp.flip(upstream, axis=1)), axis=1
    )
    adjoint = jnp.flip(flipped, axis=1)
    gate_grad = adjoint * (candidate - previous) * gate_value * retain
    candidate_grad = adjoint * gate_value
    joined = jnp.concatenate([gate_grad, candidate_grad], axis=2)
    return joined.reshape(token_count, 2 * hidden_width).astype(jnp.bfloat16)


def adamw_update(gradient, master, first_moment, second_moment):
    new_first = 0.9 * first_moment + 0.1 * gradient
    new_second = 0.95 * second_moment + 0.05 * gradient * gradient
    update = new_first / (1.0 - 0.9**10) / (jnp.sqrt(new_second / (1.0 - 0.95**10)) + 1e-08)
    new_master = master - 0.001 * (update + 0.1 * master)
    return (new_master, new_first, new_second)


def body(tokens, out_grad, weights, master, first_moment, second_moment):
    model_width = weights.shape[0]
    half_width = weights.shape[2]
    flat_weights = weights.reshape(model_width, 2 * half_width)
    gathered = lax.all_gather(tokens, "tensor", axis=0, tiled=True)
    projected = jnp.dot(gathered, flat_weights, preferred_element_type=jnp.float32)
    pre_grad = local_backward(projected, out_grad)
    replicas = lax.axis_size("dp")
    loss_scale = (gathered.shape[0] * replicas) ** (-0.5)
    input_sum = lax.psum_scatter(
        lax.dot_general(
            pre_grad, flat_weights, (((1,), (1,)), ((), ())), preferred_element_type=jnp.float32
        ).astype(jnp.bfloat16),
        "tensor",
        scatter_dimension=0,
        tiled=True,
    )
    gate_part = pre_grad[:, :half_width]
    cand_part = pre_grad[:, half_width:]
    columns = gathered
    gate_sum = lax.psum_scatter(
        lax.dot_general(
            columns, gate_part, (((0,), (0,)), ((), ())), preferred_element_type=jnp.float32
        ).astype(jnp.bfloat16),
        "dp",
        scatter_dimension=0,
        tiled=True,
    ).astype(jnp.float32)
    gate_master, gate_first, gate_second = adamw_update(
        gate_sum * loss_scale, master[:, 0], first_moment[:, 0], second_moment[:, 0]
    )
    gate_weights = lax.all_gather(gate_master.astype(jnp.bfloat16), "dp", axis=0, tiled=True)
    columns = gathered
    cand_sum = lax.psum_scatter(
        lax.dot_general(
            columns, cand_part, (((0,), (0,)), ((), ())), preferred_element_type=jnp.float32
        ).astype(jnp.bfloat16),
        "dp",
        scatter_dimension=0,
        tiled=True,
    ).astype(jnp.float32)
    cand_master, cand_first, cand_second = adamw_update(
        cand_sum * loss_scale, master[:, 1], first_moment[:, 1], second_moment[:, 1]
    )
    cand_weights = lax.all_gather(cand_master.astype(jnp.bfloat16), "dp", axis=0, tiled=True)
    new_master = jnp.stack([gate_master, cand_master], axis=1)
    new_first = jnp.stack([gate_first, cand_first], axis=1)
    new_second = jnp.stack([gate_second, cand_second], axis=1)
    new_weights = jnp.stack([gate_weights, cand_weights], axis=1)
    return (input_sum, new_weights, new_master, new_first, new_second)


def solution(mesh):
    return jax.shard_map(
        body,
        mesh=mesh,
        in_specs=(
            P(("dp", "tensor"), None),
            P("dp", "tensor"),
            P(None, None, "tensor"),
            P("dp", None, "tensor"),
            P("dp", None, "tensor"),
            P("dp", None, "tensor"),
        ),
        out_specs=(
            P(("dp", "tensor"), None),
            P(None, None, "tensor"),
            P("dp", None, "tensor"),
            P("dp", None, "tensor"),
            P("dp", None, "tensor"),
        ),
        check_vma=False,
    )
```

profile of v0, /device:TPU:0, one launch (start us, length us, event | category | flops | bytes accessed | tf_op | source)
XLA Modules:
  0.0 1105.1 jit_solution(7870390634169199136)
XLA Ops:
  26.6 17.5 %copy.27 = bf16[512,8,2,1024]{3,1,2,0:T(8,128)(2,1)} copy(bf16[512,8,2,1024]{3,2,1,0:T(2,128)(2,1)} %bitcast.98) | data formatting | bytes 33554432
  44.1 10.9 slice.543
  55.0 16.8 %slice.479 = f32[2,256,1024]{2,1,0:T(8,128)} reverse(f32[2,256,1024]{2,1,0:T(8,128)} %slice.478), dimensions={1} | reverse | bytes 4194304 | tf_op jit(solution)/shard_map/slice | solution.py:25
  71.9 10.5 slice.477
  82.4 33.9 %all-gather.4.cloned.1.call-done = bf16[1024,4096]{1,0:T(8,128)(2,1)} async-done(((bf16[512,4096]{1,0:T(8,128)(2,1)}), bf16[1024,4096]{1,0:T(8,128)(2,1)}) %all-gather.4.cloned.1.call-update) | async-done | bytes 8388624 | tf_op jit(solution)/shard_map/all_gather | solution.py:47
  116.3 21.4 %fusion.66 = f32[1024,2048]{1,0:T(8,128)S(1)} fusion(bf16[1024,4096]{1,0:T(8,128)(2,1)} %all-gather.4.cloned.1.call-done, bf16[4096,2048]{1,0:T(8,128)(2,1)} %bitcast.99), kind=kOutput, calls=%fused_computation.147 | convolution fusion | flops 17179869184 | bytes 33554432 | tf_op jit(solution)/shard_map/dot_general | solution.py:48
  176.2 16.7 %slice.482 = f32[2,256,1024]{2,1,0:T(8,128)} reverse(f32[2,256,1024]{2,1,0:T(8,128)} %slice.481), dimensions={1} | reverse | bytes 4194304 | tf_op jit(solution)/shard_map/slice | solution.py:25
  192.9 10.3 slice.475
  327.6 10.3 slice.547
  337.9 10.0 slice.611
  469.4 17.1 %slice.473 = f32[2,255,1024]{2,1,0:T(8,128)} reverse(f32[2,255,1024]{2,1,0:T(8,128)} %slice.472), dimensions={1} | reverse | bytes 4177920 | tf_op jit(solution)/shard_map/slice | solution.py:25
  507.8 10.2 pad.128
  531.1 32.8 %rev.6 = f32[2,512,1024]{2,1,0:T(8,128)} reverse(f32[2,512,1024]{2,1,0:T(8,128)} %add.291), dimensions={1} | reverse | bytes 8388608 | tf_op jit(solution)/shard_map/jit(_flip)/rev | solution.py:28
  585.1 10.2 pad.194
  614.5 14.6 %convert_bitcast_fusion = bf16[4096,1024]{0,1:T(8,128)(2,1)} fusion(bf16[1024,4096]{1,0:T(8,128)(2,1)} %all-gather.4.cloned.1.call-done, bf16[1024,2048]{1,0:T(8,128)(2,1)S(1)} %bitcast.105), kind=kOutput, calls=%fused_computation.1 | convolution fusion | flops 8594128896 | bytes 18874368 | tf_op jit(solution)/shard_map/dot_general | solution.py:77
  629.2 15.1 %convert_bitcast_fusion.1 = bf16[4096,1024]{0,1:T(8,128)(2,1)} fusion(bf16[1024,4096]{1,0:T(8,128)(2,1)} %all-gather.4.cloned.1.call-done, bf16[1024,2048]{1,0:T(8,128)(2,1)} %bitcast.106), kind=kOutput, calls=%fused_computation.2 | convolution fusion | flops 8594128896 | bytes 18874368 | tf_op jit(solution)/shard_map/dot_general | solution.py:64
  670.4 62.5 %reduce-scatter.8.cloned.1.call-done = bf16[256,1024]{0,1:T(8,128)(2,1)} async-done(((bf16[4096,1024]{0,1:T(8,128)(2,1)}), bf16[256,1024]{0,1:T(8,128)(2,1)}) %reduce-scatter.8.cloned.1.call-update) | async-done | bytes 524304 | tf_op jit(solution)/shard_map/reduce_scatter | solution.py:76
  747.3 93.0 %reduce-scatter.6.cloned.1.call-done = bf16[256,1024]{0,1:T(8,128)(2,1)} async-done(((bf16[4096,1024]{0,1:T(8,128)(2,1)}), bf16[256,1024]{0,1:T(8,128)(2,1)}) %reduce-scatter.6.cloned.1.call-update) | async-done | bytes 524304 | tf_op jit(solution)/shard_map/reduce_scatter | solution.py:63
  844.7 22.4 %convolution_convert_fusion = bf16[1024,4096]{1,0:T(8,128)(2,1)} fusion(bf16[4096,2048]{1,0:T(8,128)(2,1)} %bitcast.100, bf16[1024,1024]{1,0:T(8,128)(2,1)} %bitcast.102, bf16[1024,1024]{1,0:T(8,128)(2,1)S(1)} %bitcast.101), kind=kOutput, calls=%fused_computation.3 | convolution fusion | flops 17192452096 | bytes 29360128 | tf_op jit(solution)/shard_map/dot_general | solution.py:53
  882.1 37.6 %all-gather.8.cloned.1.call-done = bf16[4096,1024]{0,1:T(8,128)(2,1)} async-done(((bf16[256,1024]{0,1:T(8,128)(2,1)}), bf16[4096,1024]{0,1:T(8,128)(2,1)}) %all-gather.8.cloned.1.call-update) | async-done | bytes 8388624 | tf_op jit(solution)/shard_map/all_gather | solution.py:87
  919.7 77.9 %all-gather.6.cloned.1.call-done = bf16[4096,1024]{0,1:T(8,128)(2,1)} async-done(((bf16[256,1024]{0,1:T(8,128)(2,1)}), bf16[4096,1024]{0,1:T(8,128)(2,1)}) %all-gather.6.cloned.1.call-update) | async-done | bytes 8388624 | tf_op jit(solution)/shard_map/all_gather | solution.py:74
  997.6 13.9 %pad_maximum_fusion = bf16[4096,2,1024]{0,2,1:T(8,128)(2,1)} fusion(bf16[4096,1,1024]{0,2,1:T(8,128)(2,1)} %bitcast.103, bf16[4096,1,1024]{0,2,1:T(8,128)(2,1)} %bitcast.104), kind=kLoop, calls=%fused_computation | loop fusion | flops 8388608 | bytes 33554432 | tf_op jit(solution)/shard_map/stack | solution.py:91
  1011.4 41.7 %copy.17 = bf16[4096,2,1024]{2,1,0:T(2,128)(2,1)} copy(bf16[4096,2,1024]{0,2,1:T(8,128)(2,1)} %pad_maximum_fusion) | data formatting | bytes 33554432
  1053.1 44.7 %reduce-scatter.4.cloned.1.call-done = bf16[512,4096]{1,0:T(8,128)(2,1)} async-done(((bf16[1024,4096]{1,0:T(8,128)(2,1)}), bf16[512,4096]{1,0:T(8,128)(2,1)}) %reduce-scatter.4.cloned.1.call-update) | async-done | bytes 4194320 | tf_op jit(solution)/shard_map/reduce_scatter | solution.py:52
  (352 shorter events, 437.7 us)
Async XLA Ops:
  7.2 109.1 %all-gather.4.cloned.1.call-start = ((), (), s32[]{:S(2)}) async-start(), calls=%async_computation.3 | async-start | bytes 12582912 | tf_op jit(solution)/shard_map/all_gather | solution.py:47
  7.9 725.0 %reduce-scatter.8.cloned.1.call-start = ((), (), s32[]{:S(2)}) async-start(), calls=%async_computation.7 | async-start | bytes 8912896 | tf_op jit(solution)/shard_map/reduce_scatter | solution.py:76
  26.6 17.5 %copy-start.19 = (f32[2,255,1024]{2,1,0:T(8,128)S(1)}, f32[2,255,1024]{2,1,0:T(8,128)}, u32[]{:S(2)}) copy-start(f32[2,255,1024]{2,1,0:T(8,128)} %slice.542) | copy-start | bytes 6266884
  469.3 17.2 %copy-start.44 = (f32[2,2,1024]{2,1,0:T(2,128)S(1)}, f32[2,2,1024]{2,1,0:T(2,128)}, u32[]{:S(2)}) copy-start(f32[2,2,1024]{2,1,0:T(2,128)} %pad_add_fusion.1) | copy-start | bytes 49156
  469.3 17.2 %copy-start.54 = (f32[2,1,1024]{2,1,0:T(1,128)S(1)}, f32[2,1,1024]{2,1,0:T(1,128)}, u32[]{:S(2)}) copy-start(f32[2,1,1024]{2,1,0:T(1,128)} %get-tuple-element.58) | copy-start | bytes 24580
  469.4 17.2 %copy-start.55 = (f32[2,1,1024]{2,1,0:T(1,128)S(1)}, f32[2,1,1024]{2,1,0:T(1,128)}, u32[]{:S(2)}) copy-start(f32[2,1,1024]{2,1,0:T(1,128)} %get-tuple-element.59) | copy-start | bytes 24580
  469.4 17.3 %copy-start.40 = (f32[2,3,1024]{2,1,0:T(4,128)S(1)}, f32[2,3,1024]{2,1,0:T(4,128)}, u32[]{:S(2)}) copy-start(f32[2,3,1024]{2,1,0:T(4,128)} %slice.513) | copy-start | bytes 73732
  469.4 17.3 %copy-start.41 = (f32[2,3,1024]{2,1,0:T(4,128)S(1)}, f32[2,3,1024]{2,1,0:T(4,128)}, u32[]{:S(2)}) copy-start(f32[2,3,1024]{2,1,0:T(4,128)} %slice.530) | copy-start | bytes 73732
  469.4 17.3 %copy-start.51 = (f32[2,1,1024]{2,1,0:T(1,128)S(1)}, f32[2,1,1024]{2,1,0:T(1,128)}, u32[]{:S(2)}) copy-start(f32[2,1,1024]{2,1,0:T(1,128)} %slice.629) | copy-start | bytes 24580
  469.4 17.5 %copy-start.36 = (f32[2,7,1024]{2,1,0:T(8,128)S(1)}, f32[2,7,1024]{2,1,0:T(8,128)}, u32[]{:S(2)}) copy-start(f32[2,7,1024]{2,1,0:T(8,128)} %slice.532) | copy-start | bytes 172036
  469.4 17.5 %copy-start.37 = (f32[2,7,1024]{2,1,0:T(8,128)S(1)}, f32[2,7,1024]{2,1,0:T(8,128)}, u32[]{:S(2)}) copy-start(f32[2,7,1024]{2,1,0:T(8,128)} %slice.507) | copy-start | bytes 172036
  469.4 17.5 %copy-start.50 = (f32[2,1,1024]{2,1,0:T(1,128)S(1)}, f32[2,1,1024]{2,1,0:T(1,128)}, u32[]{:S(2)}) copy-start(f32[2,1,1024]{2,1,0:T(1,128)} %slice.628) | copy-start | bytes 24580
  531.1 32.9 %copy-start.56 = (f32[2,1,1024]{2,1,0:T(1,128)S(1)}, f32[2,1,1024]{2,1,0:T(1,128)}, u32[]{:S(2)}) copy-start(f32[2,1,1024]{2,1,0:T(1,128)} %get-tuple-element.54) | copy-start | bytes 24580
  531.1 32.9 %copy-start.57 = (f32[2,1,1024]{2,1,0:T(1,128)S(1)}, f32[2,1,1024]{2,1,0:T(1,128)}, u32[]{:S(2)}) copy-start(f32[2,1,1024]{2,1,0:T(1,128)} %get-tuple-element.55) | copy-start | bytes 24580
  531.1 33.0 %copy-start.42 = (f32[2,3,1024]{2,1,0:T(4,128)S(1)}, f32[2,3,1024]{2,1,0:T(4,128)}, u32[]{:S(2)}) copy-start(f32[2,3,1024]{2,1,0:T(4,128)} %slice.582) | copy-start | bytes 73732
  531.1 33.0 %copy-start.43 = (f32[2,3,1024]{2,1,0:T(4,128)S(1)}, f32[2,3,1024]{2,1,0:T(4,128)}, u32[]{:S(2)}) copy-start(f32[2,3,1024]{2,1,0:T(4,128)} %slice.599) | copy-start | bytes 73732
  531.1 33.0 %copy-start.53 = (f32[2,1,1024]{2,1,0:T(1,128)S(1)}, f32[2,1,1024]{2,1,0:T(1,128)}, u32[]{:S(2)}) copy-start(f32[2,1,1024]{2,1,0:T(1,128)} %slice.660) | copy-start | bytes 24580
  531.1 33.2 %copy-start.38 = (f32[2,7,1024]{2,1,0:T(8,128)S(1)}, f32[2,7,1024]{2,1,0:T(8,128)}, u32[]{:S(2)}) copy-start(f32[2,7,1024]{2,1,0:T(8,128)} %slice.601) | copy-start | bytes 172036
  531.1 33.2 %copy-start.39 = (f32[2,7,1024]{2,1,0:T(8,128)S(1)}, f32[2,7,1024]{2,1,0:T(8,128)}, u32[]{:S(2)}) copy-start(f32[2,7,1024]{2,1,0:T(8,128)} %slice.576) | copy-start | bytes 172036
  531.1 33.2 %copy-start.52 = (f32[2,1,1024]{2,1,0:T(1,128)S(1)}, f32[2,1,1024]{2,1,0:T(1,128)}, u32[]{:S(2)}) copy-start(f32[2,1,1024]{2,1,0:T(1,128)} %slice.659) | copy-start | bytes 24580
  629.2 211.1 %reduce-scatter.6.cloned.1.call-start = ((), (), s32[]{:S(2)}) async-start(), calls=%async_computation.5 | async-start | bytes 8912896 | tf_op jit(solution)/shard_map/reduce_scatter | solution.py:63
  644.3 275.4 %all-gather.8.cloned.1.call-start = ((), (), s32[]{:S(2)}) async-start(), calls=%async_computation.8 | async-start | bytes 8912896 | tf_op jit(solution)/shard_map/all_gather | solution.py:87
  737.3 260.3 %all-gather.6.cloned.1.call-start = ((), (), s32[]{:S(2)}) async-start(), calls=%async_computation.6 | async-start | bytes 8912896 | tf_op jit(solution)/shard_map/all_gather | solution.py:74
  844.7 253.2 %reduce-scatter.4.cloned.1.call-start = ((), (), s32[]{:S(2)}) async-start(), calls=%async_computation.4 | async-start | bytes 12582912 | tf_op jit(solution)/shard_map/reduce_scatter | solution.py:52
  (40 other events, 118.1 us)
Sparse Core Ops, SparseCore 0:
  9.5 106.6 all-gather.3
  629.3 103.5 reduce-scatter.7
  737.0 103.2 reduce-scatter.5
  842.3 77.3 all-gather.7
  921.7 75.8 all-gather.5
  1000.3 97.4 reduce-scatter.3
where the time goes:
time: 1130 us; the launch traced here: 1110 us
  local copies, waits for them, and re-layouts  552 us (49%)
  waiting for transfers between devices  350 us (31%)
  other arithmetic  114 us (10%)
  matrix products  73.4 us (6%)
  between operations  15.5 us (1%)
    slice x59, local copies, waits for them, and re-layouts, local_backward(): lax.associative_scan(linear_step, (jnp.flip(retain_next, axis=1), jnp.fli...  210 us
    slice x53, local copies, waits for them, and re-layouts, local_backward(): lax.associative_scan(linear_step, (retain, gate_value * candidate), axis=1)  139 us
    unnamed x128, local copies, waits for them, and re-layouts  110 us
    reduce_scatter x1, waiting for transfers between devices, body(): lax.psum_scatter(lax.dot_general(columns, gate_part, (((0,), (0,)), ((),...  93 us
    all_gather x1, waiting for transfers between devices, body(): lax.all_gather(gate_master.astype(jnp.bfloat16), 'dp', axis=0, tiled=True)  77.9 us
    reduce_scatter x1, waiting for transfers between devices, body(): lax.psum_scatter(lax.dot_general(columns, cand_part, (((0,), (0,)), ((),...  62.5 us
    reduce_scatter x1, waiting for transfers between devices, body(): lax.psum_scatter(lax.dot_general(pre_grad, flat_weights, (((1,), (1,)), (...  44.7 us
    mul x14, other arithmetic, linear_step(): return (earlier[0] * latter[0], latter[0] * earlier[1] + latter[1])  38.2 us
  transfers between devices with their start and end apart: 6, of which 6 were waited for; matrix products, arithmetic and copies ran while one was open for 20% of the time, Pallas kernels for 0%

commit v1 on v0

v1 whole, which is shorter than its diff:
```python
import jax
import jax.numpy as jnp
from jax import lax
from jax.experimental import pallas as pl
from jax.experimental.pallas import tpu as pltpu
from jax.sharding import PartitionSpec as P

SEQ = 512
ROWS = 8
STEP = 16
BF16 = jnp.bfloat16
F32 = jnp.float32


def scan_kernel(gate_ref, cand_ref, up_ref, out_ref, z_ref, m_ref):
    seq, width = gate_ref.shape
    half_width = out_ref.shape[1] // 2
    column = pl.multiple_of(pl.program_id(1) * width, width)
    row = lax.broadcasted_iota(jnp.int32, (ROWS, width), 0)

    def down(values, count, fill):
        return jnp.where(row >= count, pltpu.roll(values, count, 0), fill)

    def up(values, count, fill):
        return jnp.where(row < ROWS - count, pltpu.roll(values, ROWS - count, 0), fill)

    def spread(values, index):
        return jnp.broadcast_to(values[index : index + 1], (ROWS, width))

    def solve(shift, factor, term, carry):
        for count in (1, 2, 4):
            term = term + factor * shift(term, count, 0.0)
            factor = factor * shift(factor, count, 1.0)
        return term + factor * carry

    def forward(index, carry):
        start = pl.multiple_of(index * STEP, STEP)
        for part in range(STEP // ROWS):
            rows = pl.ds(start + part * ROWS, ROWS)
            z = jax.nn.sigmoid(gate_ref[rows, :])
            c = cand_ref[rows, :]
            r = 1.0 - z
            h = solve(down, r, z * c, carry)
            previous = down(h, 1, carry)
            z_ref[rows, :] = z
            m_ref[rows, :] = (c - previous) * z * r
            carry = spread(h, ROWS - 1)
        return carry

    def backward(index, carry):
        start = pl.multiple_of(seq - STEP - index * STEP, STEP)
        upstream = up_ref[pl.ds(start, STEP), :].astype(F32)
        gates, cands = [], []
        for part in reversed(range(STEP // ROWS)):
            rows = pl.ds(start + part * ROWS, ROWS)
            z = z_ref[rows, :]
            r = 1.0 - z
            u = upstream[part * ROWS : (part + 1) * ROWS]
            q = solve(up, r, r * u, carry)
            g = u + up(q, 1, carry)
            gates.insert(0, g * m_ref[rows, :])
            cands.insert(0, g * z)
            carry = spread(q, 0)
        out_ref[pl.ds(start, STEP), pl.ds(column, width)] = jnp.concatenate(gates, 0).astype(BF16)
        out_ref[pl.ds(start, STEP), pl.ds(half_width + column, width)] = jnp.concatenate(
            cands, 0
        ).astype(BF16)
        return carry

    zero = jnp.zeros((ROWS, width), F32)
    lax.fori_loop(0, seq // STEP, forward, zero, unroll=2)
    lax.fori_loop(0, seq // STEP, backward, zero, unroll=2)


def local_backward(projected, out_grad):
    tokens, both = projected.shape
    half_width = both // 2
    width = min(512, half_width)
    blocks = half_width // width
    return pl.pallas_call(
        scan_kernel,
        grid=(tokens // SEQ, blocks),
        in_specs=[
            pl.BlockSpec((SEQ, width), lambda b, j: (b, j)),
            pl.BlockSpec((SEQ, width), lambda b, j: (b, j + blocks)),
            pl.BlockSpec((SEQ, width), lambda b, j: (b, j)),
        ],
        out_specs=pl.BlockSpec((SEQ, both), lambda b, j: (b, 0)),
        out_shape=jax.ShapeDtypeStruct((tokens, both), BF16),
        scratch_shapes=[pltpu.VMEM((SEQ, width), F32), pltpu.VMEM((SEQ, width), F32)],
        cost_estimate=pl.CostEstimate(
            flops=tokens * half_width * 80, bytes_accessed=tokens * half_width * 14, transcendentals=0
        ),
    )(projected, projected, out_grad)


def adamw_update(gradient, master, first_moment, second_moment):
    new_first = 0.9 * first_moment + 0.1 * gradient
    new_second = 0.95 * second_moment + 0.05 * gradient * gradient
    update = new_first / (1.0 - 0.9**10) / (jnp.sqrt(new_second / (1.0 - 0.95**10)) + 1e-08)
    new_master = master - 0.001 * (update + 0.1 * master)
    return (new_master, new_first, new_second)


def product(a, b, contract):
    return lax.dot_general(a, b, ((contract[:1], contract[1:]), ((), ())), preferred_element_type=F32)


def body(tokens, out_grad, weights, master, first_moment, second_moment):
    model_width, _, half_width = weights.shape
    both = 2 * half_width
    flat_weights = weights.reshape(model_width, both)
    local_tokens = tokens.shape[0]
    replicas = lax.axis_size("dp")
    shards = lax.axis_size("tensor")
    shard = lax.axis_index("tensor")
    core = lax.axis_index("dp") % 2
    chips = replicas // 2
    share = model_width // replicas
    loss_scale = (local_tokens * shards * replicas) ** (-0.5)
    swap = [(i, i ^ 1) for i in range(replicas)]
    groups = [[i for i in range(replicas) if i % 2 == c] for c in range(2)]

    def columns_of(block, c):
        cut = block.reshape(block.shape[0], chips, 2, share)
        return lax.dynamic_index_in_dim(cut, c, 2, keepdims=False)

    whole = local_tokens % SEQ == 0
    if whole:
        blocks = [tokens]
        for k in range(1, shards):
            blocks.append(lax.ppermute(tokens, "tensor", [(i, (i + k) % shards) for i in range(shards)]))
        ups = [
            lax.dynamic_slice_in_dim(out_grad, ((shard - k) % shards) * local_tokens, local_tokens, 0)
            for k in range(shards)
        ]
    else:
        blocks = [lax.all_gather(tokens, "tensor", axis=0, tiled=True)]
        ups = [out_grad]

    mine_x, other_x, mine_p, other_p, terms = [], [], [], [], []
    for block, upstream in zip(blocks, ups):
        other_x.append(lax.ppermute(columns_of(block, 1 - core), "dp", swap))
        mine_x.append(columns_of(block, core))
        projected = jnp.dot(block, flat_weights, preferred_element_type=F32)
        pre_grad = local_backward(projected, upstream)
        mine_p.append(pre_grad)
        other_p.append(lax.ppermute(pre_grad, "dp", swap))
        terms.append(lambda p=pre_grad: product(p, flat_weights, (1, 1)).astype(BF16))

    parts = 1
    rows = share
    left = [jnp.concatenate([a, b], 0) for a, b in zip(mine_x, other_x)]
    right = [jnp.concatenate([a, b], 0) for a, b in zip(mine_p, other_p)]
    updated, gathered = [], []
    for part in range(parts):
        total = 0.0
        for a, b in zip(left, right):
            cut = a[:, :, part * rows : (part + 1) * rows].reshape(a.shape[0], chips * rows)
            total = total + product(cut, b, (0, 0))
        summed = lax.psum_scatter(
            total.astype(BF16), "dp", scatter_dimension=0, tiled=True, axis_index_groups=groups
        )
        gradient = (summed.astype(F32) * loss_scale).reshape(rows, 2, half_width)
        here = slice(part * rows, (part + 1) * rows)
        updated.append(adamw_update(gradient, master[here], first_moment[here], second_moment[here]))
        gathered.append(lax.all_gather(updated[-1][0].astype(BF16), "dp", axis=0, tiled=True))

    if whole:
        total = terms[0]().astype(F32)
        for k in range(1, shards):
            term = lax.ppermute(terms[k](), "tensor", [(i, (i - k) % shards) for i in range(shards)])
            total = total + term.astype(F32)
        input_grad = total.astype(BF16)
    else:
        input_grad = lax.psum_scatter(terms[0](), "tensor", scatter_dimension=0, tiled=True)

    news = [jnp.concatenate(values, 0) for values in zip(*updated)]
    return (input_grad, gathered[0], *news)


def solution(mesh):
    state = P("dp", None, "tensor")
    rows = P(("dp", "tensor"), None)
    held = P(None, None, "tensor")
    return jax.shard_map(
        body,
        mesh=mesh,
        in_specs=(rows, P("dp", "tensor"), held, state, state, state),
        out_specs=(rows, held, state, state, state),
        check_vma=False,
    )
```

time: 1130 us -> 512 us (0.45); the launches traced: 1110 us -> 512 us
  local copies, waits for them, and re-layouts: 552 us -> 63.3 us
  other arithmetic: 114 us -> 12.9 us
  waiting for transfers between devices: 350 us -> 310 us
  Pallas kernels: 0 us -> 16.8 us
  matrix products: 73.4 us -> 89.7 us
    slice x117 -> x0, local copies, waits for them, and re-layouts: 376 us -> none  [the longest x59 210 us: local_backward(): lax.associative_scan(linear_step, (jnp.flip(retain_next, axis=1), jnp.fli...]
    ppermute x0 -> x6, waiting for transfers between devices: none -> 156 us  [the longest x1 90.7 us: body(): lax.ppermute(terms[k](), 'tensor', [(i, (i - k) % shards) for i in range(...]
    all_gather x3 -> x1, waiting for transfers between devices: 149 us -> 4.91 us  [body(): lax.all_gather(updated[-1][0].astype(BF16), 'dp', axis=0, tiled=True)]
    unnamed x128 -> x9, local copies, waits for them, and re-layouts: 110 us -> 37.8 us
    reduce_scatter x3 -> x1, waiting for transfers between devices: 200 us -> 149 us  [body(): lax.psum_scatter(total.astype(BF16), 'dp', scatter_dimension=0, tiled=Tru...]
    mul x15 -> x1, other arithmetic: 42.1 us -> 2.78 us  [body(): gradient = (summed.astype(F32) * loss_scale).reshape(rows, 2, half_width)]
    add x36 -> x0, other arithmetic: 33.1 us -> none  [the longest x9 13 us: local_backward(): lax.associative_scan(linear_step, (jnp.flip(retain_next, axis=1), jnp.fli...]
    rev x1 -> x0, local copies, waits for them, and re-layouts: 32.8 us -> none  [local_backward(): adjoint = jnp.flip(flipped, axis=1)]
  transfers between devices with their start and end apart: 6 -> 8, of which waited for: 6 -> 4; matrix products, arithmetic and copies ran while one was open for 20% -> 22% of each run, Pallas kernels for 0% -> 3%
where the time goes in v1:
time: 512 us
  waiting for transfers between devices  310 us (61%)
  matrix products  89.7 us (18%)
  local copies, waits for them, and re-layouts  63.3 us (12%)
  Pallas kernels  16.8 us (3%)
  between operations  14.1 us (3%)
  other arithmetic  12.9 us (3%)
    reduce_scatter x1, waiting for transfers between devices, body(): lax.psum_scatter(total.astype(BF16), 'dp', scatter_dimension=0, tiled=Tru...  149 us
    ppermute x1, waiting for transfers between devices, body(): lax.ppermute(terms[k](), 'tensor', [(i, (i - k) % shards) for i in range(...  90.7 us
    ppermute x1, waiting for transfers between devices, body(): lax.ppermute(tokens, 'tensor', [(i, (i + k) % shards) for i in range(shar...  65.1 us
    dot_general x4, matrix products, product(): lax.dot_general(a, b, ((contract[:1], contract[1:]), ((), ())), preferred...  59.9 us
    unnamed x9, local copies, waits for them, and re-layouts  37.8 us
    dot_general x2, matrix products, body(): projected = jnp.dot(block, flat_weights, preferred_element_type=F32)  29.8 us
    pallas_call x2, Pallas kernels, local_backward(): pl.pallas_call(scan_kernel, grid=(tokens // SEQ, blocks), in_specs=[pl.Bl...  16.8 us
    dynamic_slice x4, local copies, waits for them, and re-layouts, columns_of(): return lax.dynamic_index_in_dim(cut, c, 2, keepdims=False)  14 us
  transfers between devices with their start and end apart: 8, of which 4 were waited for; matrix products, arithmetic and copies ran while one was open for 22% of the time, Pallas kernels for 3%

profile of v1, /device:TPU:0, one launch (start us, length us, event | category | flops | bytes accessed | tf_op | source)
XLA Modules:
  0.0 511.8 jit_solution(11793112568832958693)
XLA Ops:
  7.2 6.4 %copy.21 = bf16[512,4096]{0,1:T(8,128)(2,1)} copy(bf16[512,4096]{1,0:T(8,128)(2,1)} %param.6) | data formatting | bytes 8388608 | tf_op args[0]
  13.6 3.0 collective-permute-start
  16.6 3.9 constant_dynamic-slice_fusion.3
  20.5 3.1 copy.23
  23.6 17.2 %copy.27 = bf16[512,8,2,1024]{3,1,2,0:T(8,128)(2,1)} copy(bf16[512,8,2,1024]{3,2,1,0:T(2,128)(2,1)} %bitcast.18) | data formatting | bytes 33554432
  42.4 65.1 %collective-permute-done = bf16[512,4096]{0,1:T(8,128)(2,1)} collective-permute-done((bf16[512,4096]{0,1:T(8,128)(2,1)}, bf16[512,4096]{0,1:T(8,128)(2,1)}, u32[]{:S(2)}, u32[]{:S(2)}) %collective-permute-start) | collective-permute-done | bytes 4194336 | tf_op jit(solution)/shard_map/ppermute | solution.py:132
  107.5 3.9 constant_dynamic-slice_fusion.1
  111.4 3.1 copy.25
  114.5 14.9 %fusion.19.gate_ref.cand_ref = f32[512,2048]{1,0:T(8,128)} fusion(bf16[512,4096]{0,1:T(8,128)(2,1)} %collective-permute-done, bf16[4096,2048]{1,0:T(8,128)(2,1)} %bitcast.19), kind=kOutput, calls=%fused_computation.32 | convolution fusion | flops 8589934592 | bytes 25165824 | tf_op jit(solution)/shard_map/dot_general | solution.py:145
  129.4 8.4 %shard_map.102 = bf16[512,2048]{1,0:T(8,128)(2,1)} custom-call(f32[512,2048]{1,0:T(8,128)} %fusion.19.gate_ref.cand_ref, f32[512,2048]{1,0:T(8,128)} %fusion.19.gate_ref.cand_ref, bf16[512,1024]{1,0:T(8,128)(2,1)} %get-tuple-element.14.up_ref), custom_call_target="tpu_custom_call" | custom-call | flops 41943040 | bytes 7340032 | tf_op jit(solution)/shard_map/pallas_call | solution.py:80
  138.3 14.9 %fusion.18.gate_ref.cand_ref = f32[512,2048]{1,0:T(8,128)} fusion(bf16[512,4096]{1,0:T(8,128)(2,1)} %param.6, bf16[4096,2048]{1,0:T(8,128)(2,1)} %bitcast.20), kind=kOutput, calls=%fused_computation.31 | convolution fusion | flops 8589934592 | bytes 25165824 | tf_op jit(solution)/shard_map/dot_general | solution.py:145
  153.2 8.4 %shard_map.101 = bf16[512,2048]{1,0:T(8,128)(2,1)} custom-call(f32[512,2048]{1,0:T(8,128)} %fusion.18.gate_ref.cand_ref, f32[512,2048]{1,0:T(8,128)} %fusion.18.gate_ref.cand_ref, bf16[512,1024]{1,0:T(8,128)(2,1)} %get-tuple-element.13.up_ref), custom_call_target="tpu_custom_call" | custom-call | flops 41943040 | bytes 7340032 | tf_op jit(solution)/shard_map/pallas_call | solution.py:80
  161.6 4.3 copy.24
  168.6 15.6 %fusion.6 = f32[2048,2048]{1,0:T(8,128)} fusion(bf16[512,2048]{0,1:T(8,128)(2,1)} %bitcast.29, bf16[512,2048]{0,1:T(8,128)(2,1)} %bitcast.25, bf16[512,2048]{1,0:T(8,128)(2,1)} %collective-permute-done.5, bf16[512,2048]{1,0:T(8,128)(2,1)} %shard_map.102), kind=kOutput, calls=%fused_computation.10 | convolution fusion | flops 8606711808 | bytes 25165824 | tf_op jit(solution)/shard_map/dot_general | solution.py:106
  184.2 15.8 %add_convert_fusion = bf16[2048,2048]{1,0:T(8,128)(2,1)} fusion(f32[2048,2048]{1,0:T(8,128)} %fusion.6, bf16[512,2048]{0,1:T(8,128)(2,1)} %bitcast.28, bf16[512,2048]{0,1:T(8,128)(2,1)S(1)} %bitcast.24, bf16[512,2048]{1,0:T(8,128)(2,1)} %collective-permute-done.3, bf16[512,2048]{1,0:T(8,128)(2,1)} %shard_map.101), kind=kOutput, calls=%fused_computation | convolution fusion | flops 8615100416 | bytes 33554432 | tf_op jit(solution)/shard_map/dot_general | solution.py:106
  200.0 149.2 %reduce-scatter.2.cloned.1.call-done = bf16[256,2048]{1,0:T(8,128)(2,1)} async-done(((bf16[2048,2048]{1,0:T(8,128)(2,1)}), bf16[256,2048]{1,0:T(8,128)(2,1)}) %reduce-scatter.2.cloned.1.call-update) | async-done | bytes 1048592 | tf_op jit(solution)/shard_map/reduce_scatter | solution.py:161
  349.2 2.8 convert_multiply_fusion
  352.0 3.0 reshape.35
  355.0 10.1 %fusion.16 = (bf16[256,2,1024]{2,1,0:T(2,128)(2,1)}, f32[256,2,1024]{2,1,0:T(2,128)}, f32[256,2,1024]{2,1,0:T(2,128)}, f32[256,2,1024]{2,1,0:T(2,128)}) fusion(f32[256,2,1024]{2,1,0:T(2,128)} %param.9, f32[256,2,1024]{2,1,0:T(2,128)S(1)} %reshape.35, f32[256,2,1024]{2,1,0:T(2,128)} %param.10, f32[256,2,1024]{2,1,0:T(2,128)} %param.11), kind=kLoop, calls=%fused_computation.30 | loop fusion | flops 8388608 | bytes 15728640 | tf_op jit(solution)/shard_map/convert_element_type | solution.py:167
  365.1 14.5 %convolution_convert_fusion = bf16[512,4096]{1,0:T(8,128)(2,1)} fusion(bf16[512,2048]{1,0:T(8,128)(2,1)} %shard_map.102, bf16[4096,2048]{1,0:T(8,128)(2,1)} %bitcast.21), kind=kOutput, calls=%fused_computation.2 | convolution fusion | flops 8592031744 | bytes 23068672 | tf_op jit(solution)/shard_map/dot_general | solution.py:106
  381.2 90.7 %collective-permute-done.1 = bf16[512,4096]{1,0:T(8,128)(2,1)S(1)} collective-permute-done((bf16[512,4096]{1,0:T(8,128)(2,1)}, bf16[512,4096]{1,0:T(8,128)(2,1)S(1)}, u32[]{:S(2)}, u32[]{:S(2)}) %collective-permute-start.1) | collective-permute-done | bytes 4194336 | tf_op jit(solution)/shard_map/ppermute | solution.py:172
  471.9 14.0 %add_convert_fusion.1 = bf16[512,4096]{1,0:T(8,128)(2,1)} fusion(bf16[512,4096]{1,0:T(8,128)(2,1)S(1)} %collective-permute-done.1, bf16[512,2048]{1,0:T(8,128)(2,1)S(1)} %copy-done.2, bf16[4096,2048]{1,0:T(8,128)(2,1)} %bitcast.22), kind=kOutput, calls=%fused_computation.1 | convolution fusion | flops 8600420352 | bytes 27262976 | tf_op jit(solution)/shard_map/dot_general | solution.py:106
  485.9 4.9 all-gather.2.cloned.1.call-done
  490.8 14.1 %copy.29 = bf16[4096,2,1024]{2,1,0:T(2,128)(2,1)} copy(bf16[4096,2,1024]{2,1,0:T(2,128)(2,1)} %all-gather.2.cloned.1.call-done) | data formatting | bytes 33554432
  (21 shorter events, 6.4 us)
Async XLA Ops:
  7.2 342.1 %reduce-scatter.2.cloned.1.call-start = ((), (), s32[]{:S(2)}) async-start(), calls=%async_computation.1 | async-start | bytes 9437184 | tf_op jit(solution)/shard_map/reduce_scatter | solution.py:161
  13.6 93.9 %collective-permute-start = (bf16[512,4096]{0,1:T(8,128)(2,1)}, bf16[512,4096]{0,1:T(8,128)(2,1)}, u32[]{:S(2)}, u32[]{:S(2)}) collective-permute-start(bf16[512,4096]{0,1:T(8,128)(2,1)} %copy.21), channel_id=1, source_target_pairs={{0,1},{1,0},{2,3},{3,2},{4,5},{5,4},{6,7},{7,6},{8,9},{9,8},{10,11... | collective-permute-start | bytes 12582920 | tf_op jit(solution)/shard_map/ppermute | solution.py:132
  23.6 137.9 %collective-permute-start.2 = (bf16[512,8,256]{2,1,0:T(8,128)(2,1)}, bf16[512,8,256]{2,1,0:T(8,128)(2,1)}, u32[]{:S(2)}, u32[]{:S(2)}) collective-permute-start(bf16[512,8,256]{2,1,0:T(8,128)(2,1)} %bitcast.26), channel_id=1, source_target_pairs={{0,2},{2,0},{4,6},{6,4},{8,10},{10,8},{12,14},{14,12},{16,18},{18,... | collective-permute-start | bytes 6291464 | tf_op jit(solution)/shard_map/ppermute | solution.py:143
  23.6 17.2 %copy-start.1 = (bf16[1024,1024]{1,0:T(8,128)(2,1)S(1)}, bf16[1024,1024]{1,0:T(8,128)(2,1)}, u32[]{:S(2)}) copy-start(bf16[1024,1024]{1,0:T(8,128)(2,1)} %param.7) | copy-start | bytes 6291460
  114.5 51.4 %collective-permute-start.4 = (bf16[512,8,256]{2,1,0:T(8,128)(2,1)}, bf16[512,8,256]{2,1,0:T(8,128)(2,1)S(1)}, u32[]{:S(2)}, u32[]{:S(2)}) collective-permute-start(bf16[512,8,256]{2,1,0:T(8,128)(2,1)} %bitcast.27), channel_id=1, source_target_pairs={{0,2},{2,0},{4,6},{6,4},{8,10},{10,8},{12,14},{14,12},{16,18},{18,... | collective-permute-start | bytes 6291464 | tf_op jit(solution)/shard_map/ppermute | solution.py:143
  137.8 30.8 %collective-permute-start.5 = (bf16[512,2048]{1,0:T(8,128)(2,1)}, bf16[512,2048]{1,0:T(8,128)(2,1)}, u32[]{:S(2)}, u32[]{:S(2)}) collective-permute-start(bf16[512,2048]{1,0:T(8,128)(2,1)} %shard_map.102), channel_id=1, source_target_pairs={{0,2},{2,0},{4,6},{6,4},{8,10},{10,8},{12,14},{14,12},{16,18},{18,... | collective-permute-start | bytes 6291464 | tf_op jit(solution)/shard_map/ppermute | solution.py:148
  161.6 22.6 %collective-permute-start.3 = (bf16[512,2048]{1,0:T(8,128)(2,1)}, bf16[512,2048]{1,0:T(8,128)(2,1)}, u32[]{:S(2)}, u32[]{:S(2)}) collective-permute-start(bf16[512,2048]{1,0:T(8,128)(2,1)} %shard_map.101), channel_id=1, source_target_pairs={{0,2},{2,0},{4,6},{6,4},{8,10},{10,8},{12,14},{14,12},{16,18},{18,... | collective-permute-start | bytes 6291464 | tf_op jit(solution)/shard_map/ppermute | solution.py:148
  168.6 15.6 %copy-start = (bf16[512,8,1,256]{0,3,2,1:T(8,128)(2,1)S(1)}, bf16[512,8,1,256]{0,3,2,1:T(8,128)(2,1)}, u32[]{:S(2)}) copy-start(bf16[512,8,1,256]{0,3,2,1:T(8,128)(2,1)} %get-tuple-element.9) | copy-start | bytes 6291460
  200.0 290.9 %all-gather.2.cloned.1.call-start = ((), (), s32[]{:S(2)}) async-start(), calls=%async_computation.2 | async-start | bytes 17825792 | tf_op jit(solution)/shard_map/all_gather | solution.py:167
  365.1 106.8 %copy-start.2 = (bf16[512,2048]{1,0:T(8,128)(2,1)S(1)}, bf16[512,2048]{1,0:T(8,128)(2,1)}, u32[]{:S(2)}) copy-start(bf16[512,2048]{1,0:T(8,128)(2,1)} %shard_map.101) | copy-start | bytes 6291460
  379.7 92.2 %collective-permute-start.1 = (bf16[512,4096]{1,0:T(8,128)(2,1)}, bf16[512,4096]{1,0:T(8,128)(2,1)S(1)}, u32[]{:S(2)}, u32[]{:S(2)}) collective-permute-start(bf16[512,4096]{1,0:T(8,128)(2,1)} %convolution_convert_fusion), channel_id=1, source_target_pairs={{0,1},{1,0},{2,3},{3,2},{4,5},{5,4},{6,7},{7,6},{8,9},{9,8},{10,11... | collective-permute-start | bytes 12582920 | tf_op jit(solution)/shard_map/ppermute | solution.py:172
Sparse Core Ops, SparseCore 0:
  200.1 149.0 reduce-scatter.1
  365.3 125.5 all-gather.1
